TPU v7x, 32 devices: a whole 2x2x4 slice. The times are simulated.
32 devices in a mesh: head: 4 (over z), tok: 8 (over y, x, core).
Axes of the slice: x: 2, y: 2, z: 4, core: 2. Of those that a mesh axis runs over, the one named last changes fastest.
Arguments:
- video_q: bfloat16 [7168, 2048], P('tok', 'head'), may hold values from -6 to 6
- video_k: bfloat16 [7168, 2048], P('tok', 'head'), may hold values from -6 to 6
- video_v: bfloat16 [7168, 2048], P('tok', 'head'), may hold values from -6 to 6
- audio_q: bfloat16 [256, 2048], P('tok', 'head'), may hold values from -6 to 6
- audio_k: bfloat16 [256, 2048], P('tok', 'head'), may hold values from -6 to 6
- audio_v: bfloat16 [256, 2048], P('tok', 'head'), may hold values from -6 to 6
- norm_gain: float32 [2048], replicated, may hold values from 0.5 to 1.5
Outputs:
- video_out: bfloat16 [7168, 2048], P(('tok', 'head'))
- audio_out: bfloat16 [256, 2048], P('tok', 'head')
All inputs are finite; a program needn't handle non-finite values.
Results may differ from a plain program's by a relative error of at most 0.0095.
Values may be sent and summed in bfloat16 or wider, within the bound.
No kernel may reach another device: no remote copies, remote signals or barrier semaphores. Data moves between devices by JAX's collectives and lax.ppermute only.
A program may use at most 64 MiB of HBM per device.

v0:
```python
import jax
import jax.numpy as jnp
from jax import lax
from jax.sharding import PartitionSpec as P

HEAD_DIM = 64


def shards(video_q, video_k, video_v, audio_q, audio_k, audio_v, norm_gain):
    query_rows, local_width = video_q.shape
    heads_here = local_width // HEAD_DIM
    audio_rows = audio_q.shape[0]
    scaling = HEAD_DIM ** (-0.5)

    def split_heads(matrix):
        return matrix.reshape(matrix.shape[0], heads_here, HEAD_DIM)

    video_heads = split_heads(video_q)
    pieces = (
        lax.all_gather(audio_k, "tok", axis=0, tiled=True),
        lax.all_gather(audio_v, "tok", axis=0, tiled=True),
    )
    running_max = jnp.full((heads_here, query_rows), -1e30, jnp.float32)
    running_sum = jnp.zeros((heads_here, query_rows), jnp.float32)
    running_out = jnp.zeros((heads_here, query_rows, HEAD_DIM), jnp.float32)
    key_block = split_heads(pieces[0])
    value_block = split_heads(pieces[1])
    max_list = []
    sum_list = []
    out_list = []
    for absorb_head_index in range(heads_here):
        absorb_scores = (
            jnp.einsum(
                "qd,kd->qk",
                video_heads[:, absorb_head_index],
                key_block[:, absorb_head_index],
                preferred_element_type=jnp.float32,
            )
            * scaling
        )
        new_max = jnp.maximum(running_max[absorb_head_index], jnp.max(absorb_scores, axis=1))
        absorb_weights = jnp.exp(absorb_scores - new_max[:, None])
        factor = jnp.exp(running_max[absorb_head_index] - new_max)
        sum_list.append(running_sum[absorb_head_index] * factor + jnp.sum(absorb_weights, axis=1))
        out_list.append(
            running_out[absorb_head_index] * factor[:, None]
            + jnp.dot(
                absorb_weights.astype(jnp.bfloat16),
                value_block[:, absorb_head_index],
                preferred_element_type=jnp.float32,
            )
        )
        max_list.append(new_max)
    final_sum = jnp.stack(sum_list)
    final_out = jnp.stack(out_list)
    video_attn = (
        (final_out / final_sum[:, :, None]).transpose(1, 0, 2).reshape(query_rows, local_width)
    )
    video_attn = video_attn.astype(jnp.bfloat16)
    head_count = lax.axis_size("head")
    pieces = video_attn.reshape(head_count, query_rows // head_count, local_width)
    received = lax.all_to_all(pieces, "head", split_axis=0, concat_axis=2, tiled=True)
    normalize_received = received[0]
    widened = normalize_received.astype(jnp.float32)
    mean_square = jnp.mean(widened * widened, axis=-1, keepdims=True)
    video_out = (widened * lax.rsqrt(mean_square + 1e-06) * norm_gain).astype(jnp.bfloat16)
    all_queries = split_heads(lax.all_gather(audio_q, "tok", axis=0, tiled=True))
    video_keys = split_heads(video_k)
    video_values = split_heads(video_v)
    max_list, sum_list, out_list = ([], [], [])
    for head_index in range(heads_here):
        scores = (
            jnp.einsum(
                "qd,kd->qk",
                all_queries[:, head_index],
                video_keys[:, head_index],
                preferred_element_type=jnp.float32,
            )
            * scaling
        )
        local_max = jnp.max(scores, axis=1)
        weights = jnp.exp(scores - local_max[:, None])
        max_list.append(local_max)
        sum_list.append(jnp.sum(weights, axis=1))
        out_list.append(
            jnp.dot(
                weights.astype(jnp.bfloat16),
                video_values[:, head_index],
                preferred_element_type=jnp.float32,
            )
        )
    part_max = jnp.stack(max_list)
    part_sum = jnp.stack(sum_list)
    part_out = jnp.stack(out_list)
    tok_count = lax.axis_size("tok")
    grouped_max = part_max.reshape(heads_here, tok_count, audio_rows)
    grouped_sum = part_sum.reshape(heads_here, tok_count, audio_rows)
    grouped_out = part_out.reshape(heads_here, tok_count, audio_rows, HEAD_DIM)
    got_max, got_sum, got_out = (
        lax.all_to_all(grouped_max, "tok", split_axis=1, concat_axis=1, tiled=True),
        lax.all_to_all(grouped_sum, "tok", split_axis=1, concat_axis=1, tiled=True),
        lax.all_to_all(grouped_out, "tok", split_axis=1, concat_axis=1, tiled=True),
    )
    joint_max = jnp.max(got_max, axis=1, keepdims=True)
    factor = jnp.exp(got_max - joint_max)
    own_sum = jnp.sum(got_sum * factor, axis=1)
    own_out = jnp.sum(got_out * factor[:, :, :, None], axis=1)
    audio_out = (own_out / own_sum[:, :, None]).transpose(1, 0, 2).reshape(audio_rows, local_width)
    return (video_out, audio_out.astype(jnp.bfloat16))


def solution(mesh):
    placed = (
        P("tok", "head"),
        P("tok", "head"),
        P("tok", "head"),
        P("tok", "head"),
        P("tok", "head"),
        P("tok", "head"),
        P(),
    )
    return jax.shard_map(
        shards,
        mesh=mesh,
        in_specs=placed,
        out_specs=(P(("tok", "head"), None), P("tok", "head")),
        check_vma=False,
    )
```

profile of v0, /device:TPU:2, one launch (start us, length us, event | category | flops | bytes accessed | tf_op | source)
XLA Modules:
  0.0 136.5 jit_solution(5439281923956498559)
XLA Ops:
  0.6 1.5 %copy.41 = bf16[896,512]{0,1:T(8,128)(2,1)S(1)} copy(bf16[896,512]{1,0:T(8,128)(2,1)} %param.8) | data formatting | bytes 1835008 | tf_op args[1]
  2.2 9.3 %all_gather.11 = bf16[256,512]{1,0:T(8,128)(2,1)S(1)} all-gather(bf16[32,512]{1,0:T(8,128)(2,1)S(1)} %copy-done.27), channel_id=1, replica_groups=mesh['head'=4,'tok'=8] {'tok'}, dimensions={0}, use_global_device_ids=true | all-gather | bytes 294912 | tf_op jit(solution)/shard_map/all_gather | solution.py:67
  11.6 1.3 fusion.91
  14.2 1.3 fusion.93
  16.7 1.3 fusion.95
  23.2 3.8 %all-to-all-start.2 = ((f32[8,1,256]{2,1,0:T(1,128)}), f32[8,1,256]{2,1,0:T(1,128)S(1)}, u32[]{:S(2)}, u32[]{:S(2)}) async-start(f32[8,1,256]{2,1,0:T(1,128)} %reshape.485), calls=%async_computation.2 | async-start | bytes 16384 | tf_op jit(solution)/shard_map/all_to_all | solution.py:100
  26.9 9.3 %all_gather.9 = bf16[256,512]{1,0:T(8,128)(2,1)S(1)} all-gather(bf16[32,512]{1,0:T(8,128)(2,1)S(1)} %copy-done.28), channel_id=1, replica_groups=mesh['head'=4,'tok'=8] {'tok'}, dimensions={0}, use_global_device_ids=true | all-gather | bytes 294912 | tf_op jit(solution)/shard_map/all_gather | solution.py:20
  38.6 1.3 fusion.85
  41.2 1.3 fusion.87
  44.6 8.5 %all_gather.10 = bf16[256,512]{1,0:T(8,128)(2,1)S(1)} all-gather(bf16[32,512]{1,0:T(8,128)(2,1)S(1)} %copy-done.29), channel_id=1, replica_groups=mesh['head'=4,'tok'=8] {'tok'}, dimensions={0}, use_global_device_ids=true | all-gather | bytes 294912 | tf_op jit(solution)/shard_map/all_gather | solution.py:21
  53.3 1.5 %fusion.28 = f32[896]{0:T(1024)S(1)} fusion(f32[896,256]{0,1:T(8,128)} %get-tuple-element.39, f32[896]{0:T(1024)S(1)} %broadcast_maximum_fusion.6), kind=kLoop, calls=%fused_computation.81 | loop fusion | flops 457856 | bytes 924672 | tf_op jit(solution)/shard_map/reduce_sum | solution.py:44
  54.7 1.3 fusion.30
  60.6 1.6 %fusion.44 = (f32[256]{0:T(256)}, bf16[256,896]{1,0:T(8,128)(2,1)}) fusion(f32[256,896]{1,0:T(8,128)S(1)} %copy-done.13, f32[256]{0:T(256)S(1)} %copy-done.48), kind=kLoop, calls=%fused_computation.97 | loop fusion | flops 687872 | bytes 1378304 | tf_op jit(solution)/shard_map/reduce_sum | solution.py:84
  62.2 1.6 %fusion.46 = (f32[256]{0:T(256)}, bf16[256,896]{1,0:T(8,128)(2,1)}) fusion(f32[256,896]{1,0:T(8,128)S(1)} %copy-done.12, f32[256]{0:T(256)S(1)} %copy-done.46), kind=kLoop, calls=%fused_computation.99 | loop fusion | flops 687872 | bytes 1378304 | tf_op jit(solution)/shard_map/reduce_sum | solution.py:84
  63.8 1.6 %fusion.48 = (f32[256]{0:T(256)}, bf16[256,896]{1,0:T(8,128)(2,1)}) fusion(f32[256,896]{1,0:T(8,128)S(1)} %copy-done.11, f32[256]{0:T(256)S(1)} %copy-done.44), kind=kLoop, calls=%fused_computation.101 | loop fusion | flops 687872 | bytes 1378304 | tf_op jit(solution)/shard_map/reduce_sum | solution.py:84
  65.4 1.5 %fusion.50 = (f32[256]{0:T(256)}, bf16[256,896]{1,0:T(8,128)(2,1)}) fusion(f32[256,896]{1,0:T(8,128)S(1)} %copy-done.10, f32[256]{0:T(256)S(1)} %copy-done.42), kind=kLoop, calls=%fused_computation.103 | loop fusion | flops 687872 | bytes 1378304 | tf_op jit(solution)/shard_map/reduce_sum | solution.py:84
  67.0 1.6 %fusion.52 = (f32[256]{0:T(256)}, bf16[256,896]{1,0:T(8,128)(2,1)}) fusion(f32[256,896]{1,0:T(8,128)S(1)} %copy-done.9, f32[256]{0:T(256)S(1)} %copy-done.40), kind=kLoop, calls=%fused_computation.105 | loop fusion | flops 687872 | bytes 1378304 | tf_op jit(solution)/shard_map/reduce_sum | solution.py:84
  68.6 1.6 %fusion.54 = (f32[256]{0:T(256)}, bf16[256,896]{1,0:T(8,128)(2,1)}) fusion(f32[256,896]{1,0:T(8,128)S(1)} %copy-done.8, f32[256]{0:T(256)S(1)} %copy-done.38), kind=kLoop, calls=%fused_computation.107 | loop fusion | flops 687872 | bytes 1378304 | tf_op jit(solution)/shard_map/reduce_sum | solution.py:84
  70.2 1.5 %fusion.56 = (f32[256]{0:T(256)}, bf16[256,896]{1,0:T(8,128)(2,1)}) fusion(f32[256,896]{1,0:T(8,128)S(1)} %copy-done.7, f32[256]{0:T(256)S(1)} %copy-done.36), kind=kLoop, calls=%fused_computation.109 | loop fusion | flops 687872 | bytes 1378304 | tf_op jit(solution)/shard_map/reduce_sum | solution.py:84
  71.7 2.2 %copy.42 = bf16[896,512]{0,1:T(8,128)(2,1)} copy(bf16[896,512]{1,0:T(8,128)(2,1)} %param.9) | data formatting | bytes 1835008 | tf_op args[2]
  73.9 1.6 %fusion.16 = f32[8,896,64]{1,2,0:T(8,128)S(1)} fusion(f32[896,256]{0,1:T(8,128)} %copy-done.5, f32[896]{0:T(1024)S(1)} %broadcast_maximum_fusion.7, f32[896]{0:T(1024)S(1)} %get-tuple-element.35, bf16[256,8,64]{0,2,1:T(8,128)(2,1)S(1)} %bitcast.365), kind=kOutput, calls=%fused_computation.44 | convolution fusion | flops 29876224 | bytes 1187840 | tf_op jit(solution)/shard_map/dot_general | solution.py:47
  75.5 1.5 %fusion.14 = f32[8,896,64]{1,2,0:T(8,128)S(1)} fusion(f32[8,896,64]{1,2,0:T(8,128)S(1)} %fusion.16, f32[896,256]{0,1:T(8,128)} %get-tuple-element.39, f32[896]{0:T(1024)S(1)} %broadcast_maximum_fusion.6, f32[896]{0:T(1024)S(1)} %get-tuple-element.33, bf16[256,8,64]{0,2,1:T(8,128)(2,1)S(1)} %bitcast.366), kind=kOutput, calls=%fused_computation.41 | convolution fusion | flops 29876224 | bytes 1187840 | tf_op jit(solution)/shard_map/dot_general | solution.py:47
  83.7 4.7 %all-to-all-start.3 = ((f32[8,1,256]{2,1,0:T(1,128)}), f32[8,1,256]{2,1,0:T(1,128)S(1)}, u32[]{:S(2)}, u32[]{:S(2)}) async-start(f32[8,1,256]{2,1,0:T(1,128)} %reshape.487), calls=%async_computation.3 | async-start | bytes 16384 | tf_op jit(solution)/shard_map/all_to_all | solution.py:101
  88.7 1.5 %reshape.483 = f32[8,1,16384]{2,1,0:T(1,128)} reshape(f32[8,8,32,64]{3,2,1,0:T(8,128)S(1)} %bitcast.332) | data formatting | bytes 1048576
  90.2 1.5 %all-to-all-done.3 = f32[8,1,256]{2,1,0:T(1,128)S(1)} async-done(((f32[8,1,256]{2,1,0:T(1,128)}), f32[8,1,256]{2,1,0:T(1,128)S(1)}, u32[]{:S(2)}, u32[]{:S(2)}) %all-to-all-start.3) | async-done | bytes 8224 | tf_op jit(solution)/shard_map/all_to_all | solution.py:101
  91.7 4.9 %all-to-all-start.1 = ((f32[8,1,16384]{2,1,0:T(1,128)}), f32[8,1,16384]{2,1,0:T(1,128)S(1)}, u32[]{:S(2)}, u32[]{:S(2)}) async-start(f32[8,1,16384]{2,1,0:T(1,128)} %reshape.483), calls=%async_computation.1 | async-start | bytes 1048576 | tf_op jit(solution)/shard_map/all_to_all | solution.py:102
  97.6 1.7 %fusion.25 = bf16[896,8,64]{0,2,1:T(8,128)(2,1)S(1)} fusion(f32[8,896,64]{1,2,0:T(8,128)} %fusion.2, f32[8,896]{1,0:T(8,128)S(1)} %stack.112), kind=kLoop, calls=%fused_computation.78 | loop fusion | flops 917504 | bytes 2781184 | tf_op jit(solution)/shard_map/convert_element_type | solution.py:59
  100.1 1.4 %copy.38 = bf16[4,224,512]{2,1,0:T(8,128)(2,1)} copy(bf16[4,224,512]{1,0,2:T(4,128)(2,1)S(1)} %convert_element_type.94) | data formatting | bytes 1835008 | tf_op jit(solution)/shard_map/convert_element_type | solution.py:59
  101.5 3.4 %all-to-all-done.1 = f32[8,1,16384]{2,1,0:T(1,128)S(1)} async-done(((f32[8,1,16384]{2,1,0:T(1,128)}), f32[8,1,16384]{2,1,0:T(1,128)S(1)}, u32[]{:S(2)}, u32[]{:S(2)}) %all-to-all-start.1) | async-done | bytes 524320 | tf_op jit(solution)/shard_map/all_to_all | solution.py:102
  104.9 4.9 %all-to-all-start = ((bf16[4,224,512]{2,1,0:T(8,128)(2,1)}), bf16[4,224,512]{2,1,0:T(8,128)(2,1)S(1)}, u32[]{:S(2)}, u32[]{:S(2)}) async-start(bf16[4,224,512]{2,1,0:T(8,128)(2,1)} %copy.38), calls=%async_computation | async-start | bytes 1835008 | tf_op jit(solution)/shard_map/all_to_all | solution.py:62
  111.8 1.9 %reduce.5 = f32[8,16384]{1,0:T(8,128)S(1)} reduce(f32[8,1,16384]{2,1,0:T(1,128)S(1)} %all-to-all-done.1, f32[]{:T(128)} %broadcast.428), dimensions={1}, to_apply=%all_to_all.17.reduce_sub_computation | reduce | bytes 1048580 | tf_op jit(solution)/shard_map/all_to_all | solution.py:102
  115.3 17.6 %all-to-all-done = bf16[4,224,512]{2,1,0:T(8,128)(2,1)S(1)} async-done(((bf16[4,224,512]{2,1,0:T(8,128)(2,1)}), bf16[4,224,512]{2,1,0:T(8,128)(2,1)S(1)}, u32[]{:S(2)}, u32[]{:S(2)}) %all-to-all-start) | async-done | bytes 917536 | tf_op jit(solution)/shard_map/all_to_all | solution.py:62
  (222 shorter events, 33.8 us)
Async XLA Ops:
  12.9 8.8 %copy-start.49 = (f32[256]{0:T(256)}, f32[256]{0:T(256)S(1)}, u32[]{:S(2)}) copy-start(f32[256]{0:T(256)S(1)} %get-tuple-element.52) | copy-start | bytes 3076
  14.2 7.7 %copy-start.47 = (f32[256]{0:T(256)}, f32[256]{0:T(256)S(1)}, u32[]{:S(2)}) copy-start(f32[256]{0:T(256)S(1)} %get-tuple-element.54) | copy-start | bytes 3076
  15.5 6.4 %copy-start.45 = (f32[256]{0:T(256)}, f32[256]{0:T(256)S(1)}, u32[]{:S(2)}) copy-start(f32[256]{0:T(256)S(1)} %get-tuple-element.56) | copy-start | bytes 3076
  16.7 5.3 %copy-start.43 = (f32[256]{0:T(256)}, f32[256]{0:T(256)S(1)}, u32[]{:S(2)}) copy-start(f32[256]{0:T(256)S(1)} %get-tuple-element.58) | copy-start | bytes 3076
  18.0 18.2 %copy-start.41 = (f32[256]{0:T(256)}, f32[256]{0:T(256)S(1)}, u32[]{:S(2)}) copy-start(f32[256]{0:T(256)S(1)} %get-tuple-element.60) | copy-start | bytes 3076
  18.0 9.0 %copy-start.28 = (bf16[32,512]{1,0:T(8,128)(2,1)S(1)}, bf16[32,512]{1,0:T(8,128)(2,1)}, u32[]{:S(2)}) copy-start(bf16[32,512]{1,0:T(8,128)(2,1)} %param.11) | copy-start | bytes 98308
  18.0 18.4 %copy-start.26 = (bf16[896,512]{1,0:T(8,128)(2,1)S(1)}, bf16[896,512]{1,0:T(8,128)(2,1)}, u32[]{:S(2)}) copy-start(bf16[896,512]{1,0:T(8,128)(2,1)} %param.7) | copy-start | bytes 2752516
  19.2 17.7 %copy-start.39 = (f32[256]{0:T(256)}, f32[256]{0:T(256)S(1)}, u32[]{:S(2)}) copy-start(f32[256]{0:T(256)S(1)} %get-tuple-element.62) | copy-start | bytes 3076
  20.5 16.5 %copy-start.37 = (f32[256]{0:T(256)}, f32[256]{0:T(256)S(1)}, u32[]{:S(2)}) copy-start(f32[256]{0:T(256)S(1)} %get-tuple-element.64) | copy-start | bytes 3076
  21.7 15.6 %copy-start.35 = (f32[256]{0:T(256)}, f32[256]{0:T(256)S(1)}, u32[]{:S(2)}) copy-start(f32[256]{0:T(256)S(1)} %get-tuple-element.66) | copy-start | bytes 3076
  23.2 60.6 %all-to-all-start.2 = ((f32[8,1,256]{2,1,0:T(1,128)}), f32[8,1,256]{2,1,0:T(1,128)S(1)}, u32[]{:S(2)}, u32[]{:S(2)}) async-start(f32[8,1,256]{2,1,0:T(1,128)} %reshape.485), calls=%async_computation.2 | async-start | bytes 16384 | tf_op jit(solution)/shard_map/all_to_all | solution.py:100
  37.0 5.8 %copy-start.6 = (bf16[896,512]{0,1:T(8,128)(2,1)}, bf16[896,512]{0,1:T(8,128)(2,1)S(1)}, u32[]{:S(2)}) copy-start(bf16[896,512]{0,1:T(8,128)(2,1)S(1)} %copy.35) | copy-start | bytes 2752516
  37.3 7.0 %copy-start.5 = (f32[896,256]{0,1:T(8,128)}, f32[896,256]{0,1:T(8,128)S(1)}, u32[]{:S(2)}) copy-start(f32[896,256]{0,1:T(8,128)S(1)} %get-tuple-element.37) | copy-start | bytes 2752516
  53.2 4.2 %copy-start = (f32[896,256]{0,1:T(8,128)S(1)}, f32[896,256]{0,1:T(8,128)}, u32[]{:S(2)}) copy-start(f32[896,256]{0,1:T(8,128)} %get-tuple-element.45) | copy-start | bytes 2752516
  59.8 4.1 %copy-start.11 = (f32[256,896]{1,0:T(8,128)S(1)}, f32[256,896]{1,0:T(8,128)}, u32[]{:S(2)}) copy-start(f32[256,896]{1,0:T(8,128)} %get-tuple-element.59) | copy-start | bytes 2752516
  60.6 4.8 %copy-start.10 = (f32[256,896]{1,0:T(8,128)S(1)}, f32[256,896]{1,0:T(8,128)}, u32[]{:S(2)}) copy-start(f32[256,896]{1,0:T(8,128)} %get-tuple-element.61) | copy-start | bytes 2752516
  60.6 4.8 %copy-start.42 = (f32[256]{0:T(256)S(1)}, f32[256]{0:T(256)}, u32[]{:S(2)}) copy-start(f32[256]{0:T(256)} %copy-done.41) | copy-start | bytes 3076
  62.2 4.8 %copy-start.9 = (f32[256,896]{1,0:T(8,128)S(1)}, f32[256,896]{1,0:T(8,128)}, u32[]{:S(2)}) copy-start(f32[256,896]{1,0:T(8,128)} %get-tuple-element.63) | copy-start | bytes 2752516
  62.2 4.8 %copy-start.40 = (f32[256]{0:T(256)S(1)}, f32[256]{0:T(256)}, u32[]{:S(2)}) copy-start(f32[256]{0:T(256)} %copy-done.39) | copy-start | bytes 3076
  63.8 4.8 %copy-start.8 = (f32[256,896]{1,0:T(8,128)S(1)}, f32[256,896]{1,0:T(8,128)}, u32[]{:S(2)}) copy-start(f32[256,896]{1,0:T(8,128)} %get-tuple-element.65) | copy-start | bytes 2752516
  63.8 4.8 %copy-start.38 = (f32[256]{0:T(256)S(1)}, f32[256]{0:T(256)}, u32[]{:S(2)}) copy-start(f32[256]{0:T(256)} %copy-done.37) | copy-start | bytes 3076
  65.4 4.7 %copy-start.7 = (f32[256,896]{1,0:T(8,128)S(1)}, f32[256,896]{1,0:T(8,128)}, u32[]{:S(2)}) copy-start(f32[256,896]{1,0:T(8,128)} %get-tuple-element.67) | copy-start | bytes 2752516
  65.4 4.7 %copy-start.36 = (f32[256]{0:T(256)S(1)}, f32[256]{0:T(256)}, u32[]{:S(2)}) copy-start(f32[256]{0:T(256)} %copy-done.35) | copy-start | bytes 3076
  80.0 8.5 %copy-start.30 = (f32[896]{0:T(1024)S(1)}, f32[896]{0:T(1024)}, u32[]{:S(2)}) copy-start(f32[896]{0:T(1024)} %get-tuple-element.30) | copy-start | bytes 10756
  80.0 8.5 %copy-start.31 = (f32[896]{0:T(1024)S(1)}, f32[896]{0:T(1024)}, u32[]{:S(2)}) copy-start(f32[896]{0:T(1024)} %get-tuple-element.28) | copy-start | bytes 10756
  80.0 8.5 %copy-start.32 = (f32[896]{0:T(1024)S(1)}, f32[896]{0:T(1024)}, u32[]{:S(2)}) copy-start(f32[896]{0:T(1024)} %get-tuple-element.26) | copy-start | bytes 10756
  80.0 8.6 %copy-start.33 = (f32[896]{0:T(1024)S(1)}, f32[896]{0:T(1024)}, u32[]{:S(2)}) copy-start(f32[896]{0:T(1024)} %get-tuple-element.24) | copy-start | bytes 10756
  80.0 8.6 %copy-start.34 = (f32[896]{0:T(1024)S(1)}, f32[896]{0:T(1024)}, u32[]{:S(2)}) copy-start(f32[896]{0:T(1024)} %get-tuple-element.22) | copy-start | bytes 10756
  82.1 6.5 %copy-start.25 = (f32[8,8,32,64]{3,2,1,0:T(8,128)S(1)}, f32[8,8,32,64]{3,2,1,0:T(8,128)}, u32[]{:S(2)}) copy-start(f32[8,8,32,64]{3,2,1,0:T(8,128)} %copy-done.24) | copy-start | bytes 1572868
  83.7 8.0 %all-to-all-start.3 = ((f32[8,1,256]{2,1,0:T(1,128)}), f32[8,1,256]{2,1,0:T(1,128)S(1)}, u32[]{:S(2)}, u32[]{:S(2)}) async-start(f32[8,1,256]{2,1,0:T(1,128)} %reshape.487), calls=%async_computation.3 | async-start | bytes 16384 | tf_op jit(solution)/shard_map/all_to_all | solution.py:101
  91.7 13.1 %all-to-all-start.1 = ((f32[8,1,16384]{2,1,0:T(1,128)}), f32[8,1,16384]{2,1,0:T(1,128)S(1)}, u32[]{:S(2)}, u32[]{:S(2)}) async-start(f32[8,1,16384]{2,1,0:T(1,128)} %reshape.483), calls=%async_computation.1 | async-start | bytes 1048576 | tf_op jit(solution)/shard_map/all_to_all | solution.py:102
  104.9 28.0 %all-to-all-start = ((bf16[4,224,512]{2,1,0:T(8,128)(2,1)}), bf16[4,224,512]{2,1,0:T(8,128)(2,1)S(1)}, u32[]{:S(2)}, u32[]{:S(2)}) async-start(bf16[4,224,512]{2,1,0:T(8,128)(2,1)} %copy.38), calls=%async_computation | async-start | bytes 1835008 | tf_op jit(solution)/shard_map/all_to_all | solution.py:62
  (32 other events, 75.8 us)
where the time goes:
time: 137 us
  blocking collectives  27.1 us (20%)
  other arithmetic  25.6 us (19%)
  matrix products  24.9 us (18%)
  waiting for transfers between devices  22.4 us (16%)
  starting transfers between devices  18.2 us (13%)
  local copies, waits for them, and re-layouts  16.8 us (12%)
  between operations  1.52 us (1%)
    all_to_all x1, waiting for transfers between devices, shards(): lax.all_to_all(pieces, 'head', split_axis=0, concat_axis=2, tiled=True)  17.6 us
    reduce_sum x8, other arithmetic, shards(): sum_list.append(jnp.sum(weights, axis=1))  11.8 us
    dot_general x8, matrix products, shards(): jnp.einsum('qd,kd->qk', all_queries[:, head_index], video_keys[:, head_in...  10.1 us
    unnamed x130, local copies, waits for them, and re-layouts  10 us
    all_gather x1, blocking collectives, shards(): lax.all_gather(audio_q, 'tok', axis=0, tiled=True)  9.31 us
    all_gather x1, blocking collectives, shards(): lax.all_gather(audio_k, 'tok', axis=0, tiled=True)  9.26 us
    all_gather x1, blocking collectives, shards(): lax.all_gather(audio_v, 'tok', axis=0, tiled=True)  8.52 us
    dot_general x8, matrix products, shards(): jnp.einsum('qd,kd->qk', video_heads[:, absorb_head_index], key_block[:, a...  7.34 us
  transfers between devices with their start and end apart: 4, of which 3 were waited for; matrix products, arithmetic and copies ran while one was open for 36% of the time, Pallas kernels for 0%

commit v1 on v0

--- a/solution.py
+++ b/solution.py
@@ -4,6 +4,27 @@
 from jax.sharding import PartitionSpec as P
 
 HEAD_DIM = 64
+
+
+def part_the_zone(patch):
+    peer_axis = "tok"
+    v_next, carry, x_new = (lax.axis_size(peer_axis), lax.axis_index(peer_axis), patch.shape[0])
+    gallery = [q * v_next if j == 0 else q for j, q in enumerate(patch.shape)]
+    mat_out = prior = patch
+    y1 = lax.dynamic_update_slice_in_dim(
+        jnp.zeros(gallery, patch.dtype), patch, carry * x_new, axis=0
+    )
+    for j0 in range(1, v_next // 2 + 1):
+        mat_out = lax.ppermute(
+            mat_out, peer_axis, list(map(lambda j: (j, (j + 1) % v_next), range(v_next)))
+        )
+        y1 = lax.dynamic_update_slice_in_dim(y1, mat_out, (carry - j0) % v_next * x_new, axis=0)
+        if 2 * j0 < v_next:
+            prior = lax.ppermute(
+                prior, peer_axis, list(map(lambda j: (j, (j - 1) % v_next), range(v_next)))
+            )
+            y1 = lax.dynamic_update_slice_in_dim(y1, prior, (carry + j0) % v_next * x_new, axis=0)
+    return y1
 
 
 def shards(video_q, video_k, video_v, audio_q, audio_k, audio_v, norm_gain):
@@ -16,10 +37,7 @@
         return matrix.reshape(matrix.shape[0], heads_here, HEAD_DIM)
 
     video_heads = split_heads(video_q)
-    pieces = (
-        lax.all_gather(audio_k, "tok", axis=0, tiled=True),
-        lax.all_gather(audio_v, "tok", axis=0, tiled=True),
-    )
+    pieces = (lax.all_gather(audio_k, "tok", axis=0, tiled=True), part_the_zone(audio_v))
     running_max = jnp.full((heads_here, query_rows), -1e30, jnp.float32)
     running_sum = jnp.zeros((heads_here, query_rows), jnp.float32)
     running_out = jnp.zeros((heads_here, query_rows, HEAD_DIM), jnp.float32)

time: 137 us -> 165 us (1.20)
  local copies, waits for them, and re-layouts: 16.8 us -> 35.9 us
  starting transfers between devices: 18.2 us -> 28.2 us
  blocking collectives: 27.1 us -> 18.6 us
  waiting for transfers between devices: 22.4 us -> 27.5 us
  matrix products: 24.9 us -> 28.2 us
    dynamic_update_slice x0 -> x8, local copies, waits for them, and re-layouts: none -> 9.18 us  [the longest x4 4.58 us: part_the_zone(): lax.dynamic_update_slice_in_dim(y1, mat_out, (carry - j0) % v_next * x_ne...]
    all_gather x1 -> x0, blocking collectives: 8.52 us -> none  [shards(): lax.all_gather(audio_v, 'tok', axis=0, tiled=True)]
    ppermute x0 -> x7, starting transfers between devices: none -> 6.8 us  [the longest x3 4.96 us: part_the_zone(): lax.ppermute(prior, peer_axis, list(map(lambda j: (j, (j - 1) % v_next),...]
    ppermute x0 -> x7, waiting for transfers between devices: none -> 5.04 us  [the longest x4 4.71 us: part_the_zone(): lax.ppermute(mat_out, peer_axis, list(map(lambda j: (j, (j + 1) % v_next)...]
    dot_general x8, matrix products: 5.39 us -> 10.3 us  [shards(): jnp.dot(absorb_weights.astype(jnp.bfloat16), value_block[:, absorb_head_i...]
    add x8, local copies, waits for them, and re-layouts: 0.03 us -> 4.74 us  [shards(): running_sum[absorb_head_index] * factor + jnp.sum(absorb_weights, axis=1)]
    dot_general x8, matrix products: 7.34 us -> 3.59 us  [shards(): jnp.einsum('qd,kd->qk', video_heads[:, absorb_head_index], key_block[:, a...]
    reduce_sum x8, other arithmetic: 3.7 us -> 1.21 us  [shards(): jnp.sum(absorb_weights, axis=1)]
  transfers between devices with their start and end apart: 4 -> 11, of which waited for: 3 -> 6; matrix products, arithmetic and copies ran while one was open for 36% -> 50% of each run, Pallas kernels for 0% -> 0%
where the time goes in v1:
time: 165 us; the launch traced here: 164 us
  local copies, waits for them, and re-layouts  35.9 us (22%)
  starting transfers between devices  28.2 us (17%)
  matrix products  28.2 us (17%)
  waiting for transfers between devices  27.5 us (17%)
  other arithmetic  24.4 us (15%)
  blocking collectives  18.6 us (11%)
    all_to_all x1, waiting for transfers between devices, shards(): lax.all_to_all(pieces, 'head', split_axis=0, concat_axis=2, tiled=True)  16.9 us
    unnamed x141, local copies, waits for them, and re-layouts  11.8 us
    reduce_sum x8, other arithmetic, shards(): sum_list.append(jnp.sum(weights, axis=1))  10.6 us
    dot_general x8, matrix products, shards(): jnp.dot(absorb_weights.astype(jnp.bfloat16), value_block[:, absorb_head_i...  10.3 us
    dot_general x8, matrix products, shards(): jnp.einsum('qd,kd->qk', all_queries[:, head_index], video_keys[:, head_in...  10.1 us
    all_gather x1, blocking collectives, shards(): lax.all_gather(audio_q, 'tok', axis=0, tiled=True)  9.31 us
    all_gather x1, blocking collectives, shards(): lax.all_gather(audio_k, 'tok', axis=0, tiled=True)  9.26 us
    all_to_all x1, starting transfers between devices, shards(): lax.all_to_all(grouped_sum, 'tok', split_axis=1, concat_axis=1, tiled=True)  6.45 us
  transfers between devices with their start and end apart: 11, of which 6 were waited for; matrix products, arithmetic and copies ran while one was open for 50% of the time, Pallas kernels for 0%

profile of v1, /device:TPU:2, one launch (start us, length us, event | category | flops | bytes accessed | tf_op | source)
XLA Modules:
  0.0 164.3 jit_solution(8188500328700637177)
XLA Ops:
  1.6 1.7 %collective-permute-start.1 = (bf16[32,512]{0,1:T(8,128)(2,1)S(1)}, bf16[32,512]{0,1:T(8,128)(2,1)}, u32[]{:S(2)}, u32[]{:S(2)}) collective-permute-start(bf16[32,512]{0,1:T(8,128)(2,1)S(1)} %copy.43), channel_id=1, source_target_pairs={{0,7},{1,0},{2,1},{3,2},{4,3},{5,4},{6,5},{7,6},{8,15},{9,8},{10,9... | collective-permute-start | bytes 98312 | tf_op jit(solution)/shard_map/ppermute | solution.py:23
  3.3 1.5 copy.49
  4.9 9.3 %all_gather.7 = bf16[256,512]{1,0:T(8,128)(2,1)S(1)} all-gather(bf16[32,512]{1,0:T(8,128)(2,1)S(1)} %copy-done.40), channel_id=1, replica_groups=mesh['head'=4,'tok'=8] {'tok'}, dimensions={0}, use_global_device_ids=true | all-gather | bytes 294912 | tf_op jit(solution)/shard_map/all_gather | solution.py:85
  25.9 5.3 %all-to-all-start.2 = ((f32[8,1,256]{2,1,0:T(1,128)}), f32[8,1,256]{2,1,0:T(1,128)}, u32[]{:S(2)}, u32[]{:S(2)}) async-start(f32[8,1,256]{2,1,0:T(1,128)} %reshape.485), calls=%async_computation.2 | async-start | bytes 16384 | tf_op jit(solution)/shard_map/all_to_all | solution.py:118
  31.1 9.3 %all_gather.6 = bf16[256,512]{1,0:T(8,128)(2,1)S(1)} all-gather(bf16[32,512]{1,0:T(8,128)(2,1)S(1)} %copy-done.41), channel_id=1, replica_groups=mesh['head'=4,'tok'=8] {'tok'}, dimensions={0}, use_global_device_ids=true | all-gather | bytes 294912 | tf_op jit(solution)/shard_map/all_gather | solution.py:40
  49.8 1.6 fusion.44
  51.4 1.6 fusion.46
  53.0 1.6 fusion.48
  54.5 1.5 fusion.50
  57.1 1.6 fusion.54
  58.6 1.5 fusion.56
  60.2 2.2 %copy.50 = bf16[896,512]{0,1:T(8,128)(2,1)} copy(bf16[896,512]{1,0:T(8,128)(2,1)} %param.9) | data formatting | bytes 1835008 | tf_op args[2]
  69.0 1.4 collective-permute-start.3
  70.4 2.6 %collective-permute-done.2 = bf16[32,512]{0,1:T(8,128)(2,1)S(1)} collective-permute-done((bf16[32,512]{0,1:T(8,128)(2,1)S(1)}, bf16[32,512]{0,1:T(8,128)(2,1)S(1)}, u32[]{:S(2)}, u32[]{:S(2)}) %collective-permute-start.2) | collective-permute-done | bytes 32800 | tf_op jit(solution)/shard_map/ppermute | solution.py:18
  73.5 1.8 %collective-permute-start.5 = (bf16[32,512]{0,1:T(8,128)(2,1)S(1)}, bf16[32,512]{0,1:T(8,128)(2,1)}, u32[]{:S(2)}, u32[]{:S(2)}) collective-permute-start(bf16[32,512]{0,1:T(8,128)(2,1)S(1)} %collective-permute-done.3), channel_id=1, source_target_pairs={{0,7},{1,0},{2,1},{3,2},{4,3},{5,4},{6,5},{7,6},{8,15},{9,8},{10,9... | collective-permute-start | bytes 98312 | tf_op jit(solution)/shard_map/ppermute | solution.py:23
  75.3 2.1 %collective-permute-done.4 = bf16[32,512]{0,1:T(8,128)(2,1)S(1)} collective-permute-done((bf16[32,512]{0,1:T(8,128)(2,1)S(1)}, bf16[32,512]{0,1:T(8,128)(2,1)S(1)}, u32[]{:S(2)}, u32[]{:S(2)}) %collective-permute-start.4) | collective-permute-done | bytes 32800 | tf_op jit(solution)/shard_map/ppermute | solution.py:18
  85.6 2.3 %copy.59 = f32[8,8,32,64]{3,2,0,1:T(8,128)} copy(f32[8,8,32,64]{3,2,1,0:T(8,128)} %copy-done.24) | data formatting | bytes 1048576 | tf_op jit(solution)/shard_map/stack | solution.py:112
  87.9 2.7 %reshape.483 = f32[8,1,16384]{2,1,0:T(1,128)} reshape(f32[8,8,32,64]{3,2,1,0:T(8,128)} %bitcast.332) | data formatting | bytes 1048576
  93.0 1.6 dynamic_update_slice.25
  94.7 1.7 %dynamic_update_slice.26 = bf16[256,512]{0,1:T(8,128)(2,1)S(1)} dynamic-update-slice(bf16[256,512]{0,1:T(8,128)(2,1)S(1)} %dynamic_update_slice.25, bf16[32,512]{0,1:T(8,128)(2,1)} %collective-permute-done.1, s32[]{:T(128)S(6)} %select_n.59, s32[]{:T(128)} %constant.66.clone.1) | dynamic-update-slice | bytes 65540 | tf_op jit(solution)/shard_map/dynamic_update_slice | solution.py:26
  98.1 1.6 dynamic_update_slice.30
  99.8 1.6 dynamic_update_slice.31
  101.4 2.3 %fusion.16 = f32[8,896,64]{1,2,0:T(8,128)} fusion(f32[896,256]{0,1:T(8,128)} %copy-done.7, f32[896]{0:T(1024)S(1)} %broadcast_maximum_fusion.7, f32[896]{0:T(1024)S(1)} %copy-done.42, bf16[256,8,64]{0,2,1:T(8,128)(2,1)S(1)} %bitcast.381), kind=kOutput, calls=%fused_computation.44 | convolution fusion | flops 29876224 | bytes 1187840 | tf_op jit(solution)/shard_map/dot_general | solution.py:65
  103.7 2.2 %fusion.14 = f32[8,896,64]{1,2,0:T(8,128)} fusion(f32[8,896,64]{1,2,0:T(8,128)} %fusion.16, f32[896,256]{0,1:T(8,128)} %copy-done.6, f32[896]{0:T(1024)S(1)} %broadcast_maximum_fusion.6, f32[896]{0:T(1024)S(1)} %copy-done.43, bf16[256,8,64]{0,2,1:T(8,128)(2,1)S(1)} %bitcast.382), kind=kOutput, calls=%fused_computation.41 | convolution fusion | flops 29876224 | bytes 1187840 | tf_op jit(solution)/shard_map/dot_general | solution.py:65
  109.9 6.5 %all-to-all-start.3 = ((f32[8,1,256]{2,1,0:T(1,128)}), f32[8,1,256]{2,1,0:T(1,128)S(1)}, u32[]{:S(2)}, u32[]{:S(2)}) async-start(f32[8,1,256]{2,1,0:T(1,128)} %reshape.487), calls=%async_computation.3 | async-start | bytes 16384 | tf_op jit(solution)/shard_map/all_to_all | solution.py:119
  117.3 2.3 %all-to-all-done.3 = f32[8,1,256]{2,1,0:T(1,128)S(1)} async-done(((f32[8,1,256]{2,1,0:T(1,128)}), f32[8,1,256]{2,1,0:T(1,128)S(1)}, u32[]{:S(2)}, u32[]{:S(2)}) %all-to-all-start.3) | async-done | bytes 8224 | tf_op jit(solution)/shard_map/all_to_all | solution.py:119
  119.6 4.9 %all-to-all-start.1 = ((f32[8,1,16384]{2,1,0:T(1,128)}), f32[8,1,16384]{2,1,0:T(1,128)S(1)}, u32[]{:S(2)}, u32[]{:S(2)}) async-start(f32[8,1,16384]{2,1,0:T(1,128)} %reshape.483), calls=%async_computation.1 | async-start | bytes 1048576 | tf_op jit(solution)/shard_map/all_to_all | solution.py:120
  125.4 1.7 %fusion.25 = bf16[896,8,64]{0,2,1:T(8,128)(2,1)S(1)} fusion(f32[8,896,64]{1,2,0:T(8,128)} %fusion.2, f32[8,896]{1,0:T(8,128)S(1)} %copy-done.31), kind=kLoop, calls=%fused_computation.78 | loop fusion | flops 917504 | bytes 2781184 | tf_op jit(solution)/shard_map/convert_element_type | solution.py:77
  129.4 3.3 %all-to-all-done.1 = f32[8,1,16384]{2,1,0:T(1,128)S(1)} async-done(((f32[8,1,16384]{2,1,0:T(1,128)}), f32[8,1,16384]{2,1,0:T(1,128)S(1)}, u32[]{:S(2)}, u32[]{:S(2)}) %all-to-all-start.1) | async-done | bytes 524320 | tf_op jit(solution)/shard_map/all_to_all | solution.py:120
  132.7 4.9 %all-to-all-start = ((bf16[4,224,512]{2,1,0:T(8,128)(2,1)}), bf16[4,224,512]{2,1,0:T(8,128)(2,1)S(1)}, u32[]{:S(2)}, u32[]{:S(2)}) async-start(bf16[4,224,512]{2,1,0:T(8,128)(2,1)} %copy.46), calls=%async_computation | async-start | bytes 1835008 | tf_op jit(solution)/shard_map/all_to_all | solution.py:80
  140.3 1.9 %reduce.5 = f32[8,16384]{1,0:T(8,128)S(1)} reduce(f32[8,1,16384]{2,1,0:T(1,128)S(1)} %all-to-all-done.1, f32[]{:T(128)} %broadcast.435), dimensions={1}, to_apply=%all_to_all.17.reduce_sub_computation | reduce | bytes 1048580 | tf_op jit(solution)/shard_map/all_to_all | solution.py:120
  143.8 16.9 %all-to-all-done = bf16[4,224,512]{2,1,0:T(8,128)(2,1)S(1)} async-done(((bf16[4,224,512]{2,1,0:T(8,128)(2,1)}), bf16[4,224,512]{2,1,0:T(8,128)(2,1)S(1)}, u32[]{:S(2)}, u32[]{:S(2)}) %all-to-all-start) | async-done | bytes 917536 | tf_op jit(solution)/shard_map/all_to_all | solution.py:80
  (254 shorter events, 58.0 us)
Async XLA Ops:
  1.5 14.0 %copy-start.26 = (bf16[32,512]{0,1:T(8,128)(2,1)}, bf16[32,512]{0,1:T(8,128)(2,1)S(1)}, u32[]{:S(2)}) copy-start(bf16[32,512]{0,1:T(8,128)(2,1)S(1)} %copy.43) | copy-start | bytes 98308
  1.5 67.1 %collective-permute-start = (bf16[32,512]{0,1:T(8,128)(2,1)S(1)}, bf16[32,512]{0,1:T(8,128)(2,1)S(1)}, u32[]{:S(2)}, u32[]{:S(2)}) collective-permute-start(bf16[32,512]{0,1:T(8,128)(2,1)S(1)} %copy.43), channel_id=1, source_target_pairs={{0,1},{1,2},{2,3},{3,4},{4,5},{5,6},{6,7},{7,0},{8,9},{9,10},{10,1... | collective-permute-start | bytes 98312 | tf_op jit(solution)/shard_map/ppermute | solution.py:18
  1.6 67.4 %collective-permute-start.1 = (bf16[32,512]{0,1:T(8,128)(2,1)S(1)}, bf16[32,512]{0,1:T(8,128)(2,1)}, u32[]{:S(2)}, u32[]{:S(2)}) collective-permute-start(bf16[32,512]{0,1:T(8,128)(2,1)S(1)} %copy.43), channel_id=1, source_target_pairs={{0,7},{1,0},{2,1},{3,2},{4,3},{5,4},{6,5},{7,6},{8,15},{9,8},{10,9... | collective-permute-start | bytes 98312 | tf_op jit(solution)/shard_map/ppermute | solution.py:23
  15.6 8.9 %copy-start.56 = (f32[256]{0:T(256)}, f32[256]{0:T(256)S(1)}, u32[]{:S(2)}) copy-start(f32[256]{0:T(256)S(1)} %get-tuple-element.52) | copy-start | bytes 3076
  16.8 7.7 %copy-start.54 = (f32[256]{0:T(256)}, f32[256]{0:T(256)S(1)}, u32[]{:S(2)}) copy-start(f32[256]{0:T(256)S(1)} %get-tuple-element.54) | copy-start | bytes 3076
  20.7 10.4 %copy-start.41 = (bf16[32,512]{1,0:T(8,128)(2,1)S(1)}, bf16[32,512]{1,0:T(8,128)(2,1)}, u32[]{:S(2)}) copy-start(bf16[32,512]{1,0:T(8,128)(2,1)} %param.11) | copy-start | bytes 98308
  20.7 19.8 %copy-start.25 = (bf16[896,512]{1,0:T(8,128)(2,1)S(1)}, bf16[896,512]{1,0:T(8,128)(2,1)}, u32[]{:S(2)}) copy-start(bf16[896,512]{1,0:T(8,128)(2,1)} %param.7) | copy-start | bytes 2752516
  25.9 84.0 %all-to-all-start.2 = ((f32[8,1,256]{2,1,0:T(1,128)}), f32[8,1,256]{2,1,0:T(1,128)}, u32[]{:S(2)}, u32[]{:S(2)}) async-start(f32[8,1,256]{2,1,0:T(1,128)} %reshape.485), calls=%async_computation.2 | async-start | bytes 16384 | tf_op jit(solution)/shard_map/all_to_all | solution.py:118
  66.1 18.1 %copy-start.59 = (f32[256]{0:T(256)S(1)}, f32[256]{0:T(256)}, u32[]{:S(2)}) copy-start(f32[256]{0:T(256)} %get-tuple-element.16) | copy-start | bytes 3076
  66.1 18.2 %copy-start.60 = (f32[256]{0:T(256)S(1)}, f32[256]{0:T(256)}, u32[]{:S(2)}) copy-start(f32[256]{0:T(256)} %get-tuple-element.14) | copy-start | bytes 3076
  66.1 18.3 %copy-start.61 = (f32[256]{0:T(256)S(1)}, f32[256]{0:T(256)}, u32[]{:S(2)}) copy-start(f32[256]{0:T(256)} %get-tuple-element.12) | copy-start | bytes 3076
  66.2 18.3 %copy-start.62 = (f32[256]{0:T(256)S(1)}, f32[256]{0:T(256)}, u32[]{:S(2)}) copy-start(f32[256]{0:T(256)} %get-tuple-element.10) | copy-start | bytes 3076
  66.2 18.5 %copy-start.63 = (f32[256]{0:T(256)S(1)}, f32[256]{0:T(256)}, u32[]{:S(2)}) copy-start(f32[256]{0:T(256)} %get-tuple-element.6) | copy-start | bytes 3076
  66.2 18.6 %copy-start.64 = (f32[256]{0:T(256)S(1)}, f32[256]{0:T(256)}, u32[]{:S(2)}) copy-start(f32[256]{0:T(256)} %get-tuple-element.4) | copy-start | bytes 3076
  68.6 22.0 %copy-start.28 = (bf16[32,512]{0,1:T(8,128)(2,1)}, bf16[32,512]{0,1:T(8,128)(2,1)S(1)}, u32[]{:S(2)}) copy-start(bf16[32,512]{0,1:T(8,128)(2,1)S(1)} %collective-permute-done) | copy-start | bytes 98308
  68.6 4.4 %collective-permute-start.2 = (bf16[32,512]{0,1:T(8,128)(2,1)S(1)}, bf16[32,512]{0,1:T(8,128)(2,1)S(1)}, u32[]{:S(2)}, u32[]{:S(2)}) collective-permute-start(bf16[32,512]{0,1:T(8,128)(2,1)S(1)} %collective-permute-done), channel_id=1, source_target_pairs={{0,1},{1,2},{2,3},{3,4},{4,5},{5,6},{6,7},{7,0},{8,9},{9,10},{10,1... | collective-permute-start | bytes 98312 | tf_op jit(solution)/shard_map/ppermute | solution.py:18
  69.0 16.6 %copy-start.38 = (f32[896]{0:T(1024)}, f32[896]{0:T(1024)S(1)}, u32[]{:S(2)}) copy-start(f32[896]{0:T(1024)S(1)} %broadcast_maximum_fusion) | copy-start | bytes 10756
  69.0 4.5 %collective-permute-start.3 = (bf16[32,512]{0,1:T(8,128)(2,1)}, bf16[32,512]{0,1:T(8,128)(2,1)S(1)}, u32[]{:S(2)}, u32[]{:S(2)}) collective-permute-start(bf16[32,512]{0,1:T(8,128)(2,1)} %collective-permute-done.1), channel_id=1, source_target_pairs={{0,7},{1,0},{2,1},{3,2},{4,3},{5,4},{6,5},{7,6},{8,15},{9,8},{10,9... | collective-permute-start | bytes 98312 | tf_op jit(solution)/shard_map/ppermute | solution.py:23
  73.0 4.4 %collective-permute-start.4 = (bf16[32,512]{0,1:T(8,128)(2,1)S(1)}, bf16[32,512]{0,1:T(8,128)(2,1)S(1)}, u32[]{:S(2)}, u32[]{:S(2)}) collective-permute-start(bf16[32,512]{0,1:T(8,128)(2,1)S(1)} %collective-permute-done.2), channel_id=1, source_target_pairs={{0,1},{1,2},{2,3},{3,4},{4,5},{5,6},{6,7},{7,0},{8,9},{9,10},{10,1... | collective-permute-start | bytes 98312 | tf_op jit(solution)/shard_map/ppermute | solution.py:18
  73.5 24.6 %collective-permute-start.5 = (bf16[32,512]{0,1:T(8,128)(2,1)S(1)}, bf16[32,512]{0,1:T(8,128)(2,1)}, u32[]{:S(2)}, u32[]{:S(2)}) collective-permute-start(bf16[32,512]{0,1:T(8,128)(2,1)S(1)} %collective-permute-done.3), channel_id=1, source_target_pairs={{0,7},{1,0},{2,1},{3,2},{4,3},{5,4},{6,5},{7,6},{8,15},{9,8},{10,9... | collective-permute-start | bytes 98312 | tf_op jit(solution)/shard_map/ppermute | solution.py:23
  77.4 22.4 %collective-permute-start.6 = (bf16[32,512]{0,1:T(8,128)(2,1)S(1)}, bf16[32,512]{0,1:T(8,128)(2,1)}, u32[]{:S(2)}, u32[]{:S(2)}) collective-permute-start(bf16[32,512]{0,1:T(8,128)(2,1)S(1)} %collective-permute-done.4), channel_id=1, source_target_pairs={{0,1},{1,2},{2,3},{3,4},{4,5},{5,6},{6,7},{7,0},{8,9},{9,10},{10,1... | collective-permute-start | bytes 98312 | tf_op jit(solution)/shard_map/ppermute | solution.py:18
  87.9 8.4 %copy-start.30 = (bf16[32,512]{0,1:T(8,128)(2,1)S(1)}, bf16[32,512]{0,1:T(8,128)(2,1)}, u32[]{:S(2)}) copy-start(bf16[32,512]{0,1:T(8,128)(2,1)} %copy-done.29) | copy-start | bytes 98308
  91.6 9.9 %copy-start.42 = (f32[896]{0:T(1024)S(1)}, f32[896]{0:T(1024)}, u32[]{:S(2)}) copy-start(f32[896]{0:T(1024)} %get-tuple-element.35) | copy-start | bytes 10756
  91.6 12.1 %copy-start.43 = (f32[896]{0:T(1024)S(1)}, f32[896]{0:T(1024)}, u32[]{:S(2)}) copy-start(f32[896]{0:T(1024)} %get-tuple-element.33) | copy-start | bytes 10756
  96.3 9.6 %copy-start.44 = (f32[896]{0:T(1024)S(1)}, f32[896]{0:T(1024)}, u32[]{:S(2)}) copy-start(f32[896]{0:T(1024)} %get-tuple-element.31) | copy-start | bytes 10756
  106.9 9.4 %copy-start.48 = (f32[896]{0:T(1024)S(1)}, f32[896]{0:T(1024)}, u32[]{:S(2)}) copy-start(f32[896]{0:T(1024)} %get-tuple-element.23) | copy-start | bytes 10756
  108.9 15.6 %copy-start.39 = (f32[896]{0:T(1024)S(1)}, f32[896]{0:T(1024)}, u32[]{:S(2)}) copy-start(f32[896]{0:T(1024)} %copy-done.38) | copy-start | bytes 10756
  108.9 15.6 %copy-start.49 = (f32[896]{0:T(1024)S(1)}, f32[896]{0:T(1024)}, u32[]{:S(2)}) copy-start(f32[896]{0:T(1024)} %get-tuple-element.21) | copy-start | bytes 10756
  109.9 15.6 %copy-start.31 = (f32[8,896]{1,0:T(8,128)S(1)}, f32[8,896]{1,0:T(8,128)}, u32[]{:S(2)}) copy-start(f32[8,896]{1,0:T(8,128)} %stack.112) | copy-start | bytes 86020
  109.9 9.7 %all-to-all-start.3 = ((f32[8,1,256]{2,1,0:T(1,128)}), f32[8,1,256]{2,1,0:T(1,128)S(1)}, u32[]{:S(2)}, u32[]{:S(2)}) async-start(f32[8,1,256]{2,1,0:T(1,128)} %reshape.487), calls=%async_computation.3 | async-start | bytes 16384 | tf_op jit(solution)/shard_map/all_to_all | solution.py:119
  119.6 13.1 %all-to-all-start.1 = ((f32[8,1,16384]{2,1,0:T(1,128)}), f32[8,1,16384]{2,1,0:T(1,128)S(1)}, u32[]{:S(2)}, u32[]{:S(2)}) async-start(f32[8,1,16384]{2,1,0:T(1,128)} %reshape.483), calls=%async_computation.1 | async-start | bytes 1048576 | tf_op jit(solution)/shard_map/all_to_all | solution.py:120
  132.7 28.0 %all-to-all-start = ((bf16[4,224,512]{2,1,0:T(8,128)(2,1)}), bf16[4,224,512]{2,1,0:T(8,128)(2,1)S(1)}, u32[]{:S(2)}, u32[]{:S(2)}) async-start(bf16[4,224,512]{2,1,0:T(8,128)(2,1)} %copy.46), calls=%async_computation | async-start | bytes 1835008 | tf_op jit(solution)/shard_map/all_to_all | solution.py:80
  (44 other events, 159.8 us)
